TPU v7x, 128 devices: a whole 4x4x4 slice. The times are simulated.
128 devices in a mesh: grp: 4 (over x), row: 32 (over z, y, core).
Axes of the slice: x: 4, y: 4, z: 4, core: 2. Of those that a mesh axis runs over, the one named last changes fastest.
Arguments:
- snapshots: bfloat16 [8192, 131072], P(None, ('grp', 'row')), may hold values from -8 to 8
- weights: float32 [131072], P(('grp', 'row')), may hold values from 0.25 to 4
- reference_field: float32 [131072], P(('grp', 'row')), may hold values from -6 to 6
- start_basis: float32 [64, 2, 63, 8], replicated, may hold values from -6 to 6
Outputs:
- spod_modes: float32 [64, 16, 131072], P(None, None, ('grp', 'row'))
- energies: float32 [64, 8], replicated
All inputs are finite; a program needn't handle non-finite values.
Results may differ from a plain program's by a relative error of at most 0.012.
The roundings to bfloat16 on the way count: a program that leaves them out, or rounds other values in their place, can miss the bound.
Values may be sent and summed in bfloat16 or wider, within the bound.
A program may use at most 192 MiB of HBM per device.

v0:
```python
import math
import jax
import jax.numpy as jnp
from jax import lax
from jax.sharding import PartitionSpec as P

NFFT = 256
NBLK = 63
NF = 64
NM = 8
ITERS = 12
highest = lax.Precision.HIGHEST


def dft_table():
    time_steps = jnp.arange(NFFT, dtype=jnp.int32)
    freq_bins = jnp.arange(1, NF + 1, dtype=jnp.int32)
    wrapped = freq_bins[:, None] * time_steps[None, :] % NFFT
    angles = 2.0 * math.pi / NFFT * wrapped.astype(jnp.float32)
    window_taper = 0.5 - 0.5 * jnp.cos(2.0 * math.pi / NFFT * time_steps.astype(jnp.float32))
    scaled_taper = window_taper / jnp.sqrt(jnp.sum(window_taper * window_taper))
    stacked = jnp.stack([jnp.cos(angles), -jnp.sin(angles)]) * scaled_taper[None, None, :]
    return stacked.astype(jnp.bfloat16)


def apply_gram(gram_real, gram_imag, basis_real, basis_imag):
    image_real = jnp.einsum("fbc,fck->fbk", gram_real, basis_real, precision=highest) - jnp.einsum(
        "fbc,fck->fbk", gram_imag, basis_imag, precision=highest
    )
    image_imag = jnp.einsum("fbc,fck->fbk", gram_real, basis_imag, precision=highest) + jnp.einsum(
        "fbc,fck->fbk", gram_imag, basis_real, precision=highest
    )
    return (image_real, image_imag)


def orthonormalize(image_real, image_imag):
    cols_real = []
    cols_imag = []
    for column in range(image_real.shape[2]):
        target_real = image_real[:, :, column]
        target_imag = image_imag[:, :, column]
        for earlier in range(column):
            prior_real = cols_real[earlier]
            prior_imag = cols_imag[earlier]
            inner_real = jnp.sum(
                prior_real * target_real + prior_imag * target_imag, axis=1, keepdims=True
            )
            inner_imag = jnp.sum(
                prior_real * target_imag - prior_imag * target_real, axis=1, keepdims=True
            )
            target_real, target_imag = (
                target_real - (inner_real * prior_real - inner_imag * prior_imag),
                target_imag - (inner_real * prior_imag + inner_imag * prior_real),
            )
        length = jnp.sqrt(
            jnp.sum(target_real * target_real + target_imag * target_imag, axis=1, keepdims=True)
            + 1e-06
        )
        cols_real.append(target_real / length)
        cols_imag.append(target_imag / length)
    return (jnp.stack(cols_real, axis=2), jnp.stack(cols_imag, axis=2))


def subspace_solve(gram_real, gram_imag, start_basis):

    def sweep_once(sweep_index, current):
        image_real, image_imag = apply_gram(gram_real, gram_imag, current[0], current[1])
        return orthonormalize(image_real, image_imag)

    basis_real, basis_imag = lax.fori_loop(
        0, ITERS, sweep_once, (start_basis[:, 0], start_basis[:, 1])
    )
    image_real, image_imag = apply_gram(gram_real, gram_imag, basis_real, basis_imag)
    energy = jnp.sum(basis_real * image_real + basis_imag * image_imag, axis=1)
    return (basis_real, basis_imag, energy)


def coefficient_matrix(basis_real, basis_imag):
    round_real = basis_real.astype(jnp.bfloat16)
    round_imag = basis_imag.astype(jnp.bfloat16)
    upper_half = jnp.concatenate([round_real, round_imag], axis=2)
    lower_half = jnp.concatenate([-round_imag, round_real], axis=2)
    return jnp.stack([upper_half, lower_half], axis=1)


def phase_turn(correlation, energy):
    gain_scale = 1.0 / jnp.sqrt(energy + 1e-06)
    tilt_real = gain_scale * correlation[:, :NM]
    tilt_imag = gain_scale * correlation[:, NM:]
    tilt_size = jnp.sqrt(jnp.maximum(tilt_real * tilt_real + tilt_imag * tilt_imag, 0.25))
    return (gain_scale * tilt_real / tilt_size, -gain_scale * tilt_imag / tilt_size)


def finish(projected, factor_real, factor_imag, root_weight):
    part_real = projected[:, :NM]
    part_imag = projected[:, NM:]
    inverse_root = 1.0 / root_weight
    out_real = (
        part_real * factor_real[:, :, None] - part_imag * factor_imag[:, :, None]
    ) * inverse_root
    out_imag = (
        part_real * factor_imag[:, :, None] + part_imag * factor_real[:, :, None]
    ) * inverse_root
    return jnp.concatenate([out_real, out_imag], axis=1)


def shards(snapshots, weights, reference_field, start_basis):
    dft_rows = dft_table()
    half_len = NFFT // 2
    rows_here = snapshots.shape[1]
    total_rows = rows_here * lax.axis_size(("grp", "row"))
    hop_rows = snapshots.reshape(NBLK + 1, half_len, rows_here)
    root_weight = jnp.sqrt(weights)
    leading = jnp.einsum(
        "pft,htx->fphx",
        dft_rows[:, :, :half_len],
        hop_rows[:NBLK],
        preferred_element_type=jnp.float32,
    )
    trailing = jnp.einsum(
        "pft,htx->fphx", dft_rows[:, :, half_len:], hop_rows[1:], preferred_element_type=jnp.float32
    )
    coeffs = ((leading + trailing) * root_weight).astype(jnp.bfloat16)
    real_part = jnp.einsum("fpbx,fpcx->fbc", coeffs, coeffs, preferred_element_type=jnp.float32)
    cross_part = jnp.einsum(
        "fbx,fcx->fbc", coeffs[:, 0], coeffs[:, 1], preferred_element_type=jnp.float32
    )
    cross_anti = cross_part - jnp.swapaxes(cross_part, 1, 2)
    gram_part = jnp.concatenate([real_part, cross_anti], axis=2)
    probe = (root_weight * reference_field).astype(jnp.bfloat16)
    projection_part = jnp.einsum("fpbx,x->fpb", coeffs, probe, preferred_element_type=jnp.float32)
    summed = lax.psum(gram_part, ("grp", "row"))
    gram_real = summed[:, :NBLK, :NBLK] / total_rows
    gram_imag = summed[:, :NBLK, NBLK:] / total_rows
    basis_real, basis_imag, energy = subspace_solve(gram_real, gram_imag, start_basis)
    local_matrix = coefficient_matrix(basis_real, basis_imag)
    extras = energy[:, None, :]
    energies = extras[:, 0]
    projected = jnp.einsum(
        "fpbk,fpbx->fkx", local_matrix, coeffs, preferred_element_type=jnp.float32
    )
    projection = lax.psum(projection_part, ("grp", "row")) / math.sqrt(total_rows)
    correlation = jnp.einsum(
        "fpb,fpbk->fk", projection, local_matrix.astype(jnp.float32), precision=highest
    )
    factor_real, factor_imag = phase_turn(correlation, energies)
    return (finish(projected, factor_real, factor_imag, root_weight), energies)


def solution(mesh):
    in_specs = (P(None, ("grp", "row")), P(("grp", "row")), P(("grp", "row")), P())
    out_specs = (P(None, None, ("grp", "row")), P())
    return jax.shard_map(shards, mesh=mesh, in_specs=in_specs, out_specs=out_specs, check_vma=False)
```

profile of v0, /device:TPU:1, one launch (start us, length us, event | category | flops | bytes accessed | tf_op | source)
XLA Modules:
  0.0 661.7 jit_solution(498211603777411236)
XLA Ops:
  9.0 23.1 %fusion.84 = (bf16[8064,1024]{1,0:T(8,128)(2,1)}, bf16[8064,1024]{1,0:T(8,128)(2,1)}) fusion(bf16[8192,1024]{1,0:T(8,128)(2,1)} %param.6), kind=kLoop, calls=%fused_computation.327 | loop fusion | bytes 66060288 | tf_op jit(solution)/shard_map/slice | solution.py:121
  32.1 21.0 %fusion.72 = f32[2,64,63,1024]{3,1,2,0:T(8,128)} fusion(bf16[63,128,1024,1]{2,1,0,3:T(8,128)(2,1)} %bitcast.408, bf16[2,64,256]{2,1,0:T(8,128)(2,1)S(1)} %fusion.65), kind=kOutput, calls=%fused_computation.304 | convolution fusion | flops 2113929216 | bytes 49577984 | tf_op jit(solution)/shard_map/pft,htx->fphx/dot_general | solution.py:114
  53.2 23.1 %fusion.50 = bf16[64,2,63,1024]{3,0,2,1:T(8,128)(2,1)} fusion(f32[1024]{0:T(1024)S(1)} %get-tuple-element.268, f32[2,64,63,1024]{3,1,2,0:T(8,128)} %fusion.72, bf16[63,128,1024,1]{2,1,0,3:T(8,128)(2,1)} %bitcast.407, bf16[2,64,256]{2,1,0:T(8,128)(2,1)S(1)} %fusion.65), kind=kOutput, calls=%fused_computation.263 | convolution fusion | flops 2138701824 | bytes 66097152 | tf_op jit(solution)/shard_map/pft,htx->fphx/dot_general | solution.py:120
  76.3 12.3 %slice_bitcast_fusion.1 = (bf16[64,63,1024]{2,0,1:T(8,128)(2,1)}, bf16[64,63,1024]{2,0,1:T(8,128)(2,1)}) fusion(bf16[64,2,63,1024]{3,0,2,1:T(8,128)(2,1)} %fusion.50), kind=kLoop, calls=%fused_computation.268 | loop fusion | bytes 33030144 | tf_op jit(solution)/shard_map/squeeze | solution.py:126
  88.5 33.2 %fusion.57 = f32[64,63,63]{2,1,0:T(8,128)} fusion(bf16[64,2,63,1024]{3,0,2,1:T(8,128)(2,1)} %fusion.50), kind=kOutput, calls=%fused_computation.277 | convolution fusion | flops 1040449536 | bytes 17531136 | tf_op jit(solution)/shard_map/fpbx,fpcx->fbc/dot_general | solution.py:124
  121.8 14.4 %fusion.51 = f32[64,63,63]{2,1,0:T(8,128)S(1)} fusion(bf16[64,63,1024]{2,0,1:T(8,128)(2,1)} %get-tuple-element.255, bf16[64,63,1024]{2,0,1:T(8,128)(2,1)} %get-tuple-element.254), kind=kOutput, calls=%fused_computation.264 | convolution fusion | flops 520224768 | bytes 17531136 | tf_op jit(solution)/shard_map/fbx,fcx->fbc/dot_general | solution.py:125
  142.4 10.0 %fusion.74 = f32[1,64,2,63]{1,0,3,2:T(1,128)S(1)} fusion(bf16[64,2,63,1024]{3,0,2,1:T(8,128)(2,1)} %fusion.50, bf16[1024,1,1,1]{0,1,2,3:T(2,128)(2,1)S(1)} %reshape.3858), kind=kOutput, calls=%fused_computation.309 | convolution fusion | flops 16515072 | bytes 16549376 | tf_op jit(solution)/shard_map/fpbx,x->fpb/dot_general | solution.py:131
  152.5 69.7 %psum.15 = f32[64,2,63]{2,1,0:T(2,128)S(1)} all-reduce(f32[64,2,63]{2,1,0:T(2,128)S(1)} %bitcast.409), channel_id=1, replica_groups=mesh['grp'=4,'row'=32] {'grp','row'}, use_global_device_ids=true, to_apply=%region_69.70 | all-reduce | flops 8064 | bytes 64512 | tf_op jit(solution)/shard_map/psum | solution.py:142
  223.7 73.2 %all-reduce.2.cloned.1.call-done = f32[64,63,126]{2,1,0:T(8,128)} async-done(((f32[64,63,126]{2,1,0:T(8,128)}), f32[64,63,126]{2,1,0:T(8,128)}) %all-reduce.2.cloned.1.call-update) | async-done | bytes 2032144 | tf_op jit(solution)/shard_map/psum | solution.py:132
  296.8 4.4 slice_multiply_fusion
  301.2 299.5 %while.12 = (s32[]{:T(128)}, f32[64,63,8]{0,2,1:T(8,128)}, f32[64,63,8]{0,2,1:T(8,128)}, f32[64,63,63]{2,1,0:T(8,128)}, f32[64,63,63]{2,1,0:T(8,128)S(1)}, /*index=5*/s32[]{:T(128)}) while((s32[]{:T(128)}, f32[64,63,8]{0,2,1:T(8,128)}, f32[64,63,8]{0,2,1:T(8,128)}, f32[64,63,63]{2,1,0:T(8,128)}, f32[64,63,63]{2,1,0:T(8,128)S(1)}, ...), condition=%wide.region_67.68_spmd, body=%wide.region_2.67_spmd.sunk | while | flops 100723840 | bytes 13749573 | solution.py:70
  302.7 4.9 fusion.131
  312.8 4.9 fusion.134
  317.9 3.4 fusion.135
  327.7 4.9 fusion.131
  337.7 4.9 fusion.134
  342.8 3.4 fusion.135
  352.6 4.9 fusion.131
  362.6 4.9 fusion.134
  367.7 3.4 fusion.135
  377.5 4.9 fusion.131
  387.5 4.9 fusion.134
  392.6 3.4 fusion.135
  402.4 4.9 fusion.131
  412.4 4.9 fusion.134
  417.6 3.4 fusion.135
  427.3 4.9 fusion.131
  437.3 4.9 fusion.134
  442.5 3.4 fusion.135
  452.2 4.9 fusion.131
  462.3 4.9 fusion.134
  467.4 3.4 fusion.135
  477.1 4.9 fusion.131
  487.2 4.9 fusion.134
  492.3 3.4 fusion.135
  502.0 4.9 fusion.131
  512.1 4.9 fusion.134
  527.0 4.9 fusion.131
  537.0 4.9 fusion.134
  542.1 3.4 fusion.135
  551.9 4.9 fusion.131
  561.9 4.9 fusion.134
  576.8 4.9 fusion.131
  586.8 4.9 fusion.134
  603.2 4.9 fusion.80
  611.5 3.5 fusion.60
  615.0 3.6 fusion.63
  618.8 29.5 %fusion.54 = f32[64,16,1024]{2,1,0:T(8,128)} fusion(bf16[64,2,63,1024]{3,0,2,1:T(8,128)(2,1)} %fusion.50, bf16[64,1,63,16]{2,3,1,0:T(8,128)(2,1)S(1)} %get-tuple-element.263, bf16[64,1,63,16]{2,3,1,0:T(8,128)(2,1)S(1)} %get-tuple-element.262), kind=kOutput, calls=%fused_computation.270 | convolution fusion | flops 264370176 | bytes 20967424 | tf_op jit(solution)/shard_map/fpbk,fpbx->fkx/dot_general | solution.py:139
  (766 shorter events, 168.7 us)
Async XLA Ops:
  7.2 289.7 %all-reduce.2.cloned.1.call-start = ((), (), s32[]{:S(2)}) async-start(), calls=%async_computation | async-start | bytes 4194304 | tf_op jit(solution)/shard_map/psum | solution.py:132
  32.1 21.1 %copy-start.5 = (f32[1024]{0:T(1024)S(1)}, f32[1024]{0:T(1024)}, u32[]{:S(2)}) copy-start(f32[1024]{0:T(1024)} %param.8) | copy-start | bytes 12292
  32.1 21.1 %copy-start.6 = (f32[1024]{0:T(1024)S(1)}, f32[1024]{0:T(1024)}, u32[]{:S(2)}) copy-start(f32[1024]{0:T(1024)} %param.7) | copy-start | bytes 12292
  138.2 2.2 copy-start.1
  142.4 80.5 %copy-start.2 = (f32[64,2,63,8]{0,3,2,1:T(8,128)S(1)}, f32[64,2,63,8]{0,3,2,1:T(8,128)}, u32[]{:S(2)}) copy-start(f32[64,2,63,8]{0,3,2,1:T(8,128)} %param.9) | copy-start | bytes 774148
  601.9 6.3 copy-start
  618.7 30.2 %copy-start.4 = (f32[64,8]{0,1:T(8,128)}, f32[64,8]{0,1:T(8,128)S(1)}, u32[]{:S(2)}) copy-start(f32[64,8]{0,1:T(8,128)S(1)} %copy.354) | copy-start | bytes 6148
  618.8 29.5 %copy-start.3 = (f32[64,2,63]{2,1,0:T(2,128)S(1)}, f32[64,2,63]{2,1,0:T(2,128)}, u32[]{:S(2)}) copy-start(f32[64,2,63]{2,1,0:T(2,128)} %broadcast_multiply_fusion.13) | copy-start | bytes 96772
Sparse Core Ops, SparseCore 0:
  142.5 154.2 all-reduce.1
where the time goes:
time: 669 us; the launch traced here: 662 us
  matrix products  346 us (52%)
  local copies, waits for them, and re-layouts  107 us (16%)
  waiting for transfers between devices  73.2 us (11%)
  blocking collectives  69.7 us (10%)
  other arithmetic  47 us (7%)
  between operations  15.1 us (2%)
    psum x1, waiting for transfers between devices, shards(): summed = lax.psum(gram_part, ('grp', 'row'))  73.2 us
    psum x1, blocking collectives, shards(): lax.psum(projection_part, ('grp', 'row')) / math.sqrt(total_rows)  69.7 us
    dot_general x13, matrix products, apply_gram(): jnp.einsum('fbc,fck->fbk', gram_real, basis_real, precision=highest)  64.2 us
    dot_general x13, matrix products, apply_gram(): jnp.einsum('fbc,fck->fbk', gram_real, basis_imag, precision=highest)  62.7 us
    dot_general x13, matrix products, apply_gram(): jnp.einsum('fbc,fck->fbk', gram_imag, basis_real, precision=highest)  43.9 us
    dot_general x13, matrix products, apply_gram(): jnp.einsum('fbc,fck->fbk', gram_imag, basis_imag, precision=highest)  43.8 us
    dot_general x1, matrix products, shards(): jnp.einsum('fpbx,fpcx->fbc', coeffs, coeffs, preferred_element_type=jnp.f...  33.2 us
    dot_general x1, matrix products, shards(): jnp.einsum('fpbk,fpbx->fkx', local_matrix, coeffs, preferred_element_type...  29.5 us
  transfers between devices with their start and end apart: 1, of which 1 were waited for; matrix products, arithmetic and copies ran while one was open for 2% of the time, Pallas kernels for 0%

commit v1 on v0

--- a/solution.py
+++ b/solution.py
@@ -139,7 +139,7 @@
     projected = jnp.einsum(
         "fpbk,fpbx->fkx", local_matrix, coeffs, preferred_element_type=jnp.float32
     )
-    projection = lax.psum(projection_part, ("grp", "row")) / math.sqrt(total_rows)
+    projection = lax.psum(lax.psum(projection_part, "grp"), "row") / math.sqrt(total_rows)
     correlation = jnp.einsum(
         "fpb,fpbk->fk", projection, local_matrix.astype(jnp.float32), precision=highest
     )

time: 669 us -> 670 us (level)
  blocking collectives: 69.7 us -> 140 us
  waiting for transfers between devices: 73.2 us -> 3.03 us
    psum x1 -> x2, blocking collectives: 69.7 us -> 140 us  [the longest x1 125 us: shards(): lax.psum(lax.psum(projection_part, 'grp'), 'row') / math.sqrt(total_rows)]
    psum x1, waiting for transfers between devices: 73.2 us -> 3.01 us  [shards(): summed = lax.psum(gram_part, ('grp', 'row'))]
where the time goes in v1:
time: 670 us; the launch traced here: 662 us
  matrix products  346 us (52%)
  blocking collectives  140 us (21%)
  local copies, waits for them, and re-layouts  107 us (16%)
  other arithmetic  47 us (7%)
  between operations  15.1 us (2%)
    psum x1, blocking collectives, shards(): lax.psum(lax.psum(projection_part, 'grp'), 'row') / math.sqrt(total_rows)  125 us
    dot_general x13, matrix products, apply_gram(): jnp.einsum('fbc,fck->fbk', gram_real, basis_real, precision=highest)  64.2 us
    dot_general x13, matrix products, apply_gram(): jnp.einsum('fbc,fck->fbk', gram_real, basis_imag, precision=highest)  62.7 us
    dot_general x13, matrix products, apply_gram(): jnp.einsum('fbc,fck->fbk', gram_imag, basis_real, precision=highest)  43.9 us
    dot_general x13, matrix products, apply_gram(): jnp.einsum('fbc,fck->fbk', gram_imag, basis_imag, precision=highest)  43.8 us
    dot_general x1, matrix products, shards(): jnp.einsum('fpbx,fpcx->fbc', coeffs, coeffs, preferred_element_type=jnp.f...  33.2 us
    dot_general x1, matrix products, shards(): jnp.einsum('fpbk,fpbx->fkx', local_matrix, coeffs, preferred_element_type...  29.5 us
    another operation x24, local copies, waits for them, and re-layouts  26.7 us
  transfers between devices with their start and end apart: 1, of which 1 were waited for; matrix products, arithmetic and copies ran while one was open for 2% of the time, Pallas kernels for 0%

profile of v1, /device:TPU:1, one launch (start us, length us, event | category | flops | bytes accessed | tf_op | source)
XLA Modules:
  0.0 661.7 jit_solution(5132275046788033403)
XLA Ops:
  9.0 23.1 %fusion.84 = (bf16[8064,1024]{1,0:T(8,128)(2,1)}, bf16[8064,1024]{1,0:T(8,128)(2,1)}) fusion(bf16[8192,1024]{1,0:T(8,128)(2,1)} %param.6), kind=kLoop, calls=%fused_computation.327 | loop fusion | bytes 66060288 | tf_op jit(solution)/shard_map/slice | solution.py:121
  32.1 21.0 %fusion.72 = f32[2,64,63,1024]{3,1,2,0:T(8,128)} fusion(bf16[63,128,1024,1]{2,1,0,3:T(8,128)(2,1)} %bitcast.408, bf16[2,64,256]{2,1,0:T(8,128)(2,1)S(1)} %fusion.65), kind=kOutput, calls=%fused_computation.304 | convolution fusion | flops 2113929216 | bytes 49577984 | tf_op jit(solution)/shard_map/pft,htx->fphx/dot_general | solution.py:114
  53.2 23.1 %fusion.50 = bf16[64,2,63,1024]{3,0,2,1:T(8,128)(2,1)} fusion(f32[1024]{0:T(1024)S(1)} %get-tuple-element.268, f32[2,64,63,1024]{3,1,2,0:T(8,128)} %fusion.72, bf16[63,128,1024,1]{2,1,0,3:T(8,128)(2,1)} %bitcast.407, bf16[2,64,256]{2,1,0:T(8,128)(2,1)S(1)} %fusion.65), kind=kOutput, calls=%fused_computation.263 | convolution fusion | flops 2138701824 | bytes 66097152 | tf_op jit(solution)/shard_map/pft,htx->fphx/dot_general | solution.py:120
  76.3 12.3 %slice_bitcast_fusion.1 = (bf16[64,63,1024]{2,0,1:T(8,128)(2,1)}, bf16[64,63,1024]{2,0,1:T(8,128)(2,1)}) fusion(bf16[64,2,63,1024]{3,0,2,1:T(8,128)(2,1)} %fusion.50), kind=kLoop, calls=%fused_computation.268 | loop fusion | bytes 33030144 | tf_op jit(solution)/shard_map/squeeze | solution.py:126
  88.5 33.2 %fusion.57 = f32[64,63,63]{2,1,0:T(8,128)} fusion(bf16[64,2,63,1024]{3,0,2,1:T(8,128)(2,1)} %fusion.50), kind=kOutput, calls=%fused_computation.277 | convolution fusion | flops 1040449536 | bytes 17531136 | tf_op jit(solution)/shard_map/fpbx,fpcx->fbc/dot_general | solution.py:124
  121.8 14.4 %fusion.51 = f32[64,63,63]{2,1,0:T(8,128)S(1)} fusion(bf16[64,63,1024]{2,0,1:T(8,128)(2,1)} %get-tuple-element.255, bf16[64,63,1024]{2,0,1:T(8,128)(2,1)} %get-tuple-element.254), kind=kOutput, calls=%fused_computation.264 | convolution fusion | flops 520224768 | bytes 17531136 | tf_op jit(solution)/shard_map/fbx,fcx->fbc/dot_general | solution.py:125
  142.4 10.0 %fusion.74 = f32[1,64,2,63]{1,0,3,2:T(1,128)S(1)} fusion(bf16[64,2,63,1024]{3,0,2,1:T(8,128)(2,1)} %fusion.50, bf16[1024,1,1,1]{0,1,2,3:T(2,128)(2,1)S(1)} %reshape.3858), kind=kOutput, calls=%fused_computation.309 | convolution fusion | flops 16515072 | bytes 16549376 | tf_op jit(solution)/shard_map/fpbx,x->fpb/dot_general | solution.py:131
  152.5 14.6 %psum.22 = f32[64,2,63]{2,1,0:T(2,128)S(1)} all-reduce(f32[64,2,63]{2,1,0:T(2,128)S(1)} %bitcast.409), channel_id=1, replica_groups=mesh['grp'=4,'row'=32] {'grp'}, use_global_device_ids=true, to_apply=%region_69.70 | all-reduce | flops 8064 | bytes 64512 | tf_op jit(solution)/shard_map/psum | solution.py:142
  167.2 125.2 %psum.23 = f32[64,2,63]{2,1,0:T(2,128)S(1)} all-reduce(f32[64,2,63]{2,1,0:T(2,128)S(1)} %psum.22), channel_id=1, replica_groups=mesh['grp'=4,'row'=32] {'row'}, use_global_device_ids=true, to_apply=%region_70.71 | all-reduce | flops 8064 | bytes 64512 | tf_op jit(solution)/shard_map/psum | solution.py:142
  296.9 4.4 slice_multiply_fusion
  301.3 299.5 %while.12 = (s32[]{:T(128)}, f32[64,63,8]{0,2,1:T(8,128)}, f32[64,63,8]{0,2,1:T(8,128)}, f32[64,63,63]{2,1,0:T(8,128)}, f32[64,63,63]{2,1,0:T(8,128)S(1)}, /*index=5*/s32[]{:T(128)}) while((s32[]{:T(128)}, f32[64,63,8]{0,2,1:T(8,128)}, f32[64,63,8]{0,2,1:T(8,128)}, f32[64,63,63]{2,1,0:T(8,128)}, f32[64,63,63]{2,1,0:T(8,128)S(1)}, ...), condition=%wide.region_67.68_spmd, body=%wide.region_2.67_spmd.sunk | while | flops 100723840 | bytes 13749573 | solution.py:70
  302.8 4.9 fusion.131
  312.8 4.9 fusion.134
  317.9 3.4 fusion.135
  327.7 4.9 fusion.131
  337.7 4.9 fusion.134
  342.8 3.4 fusion.135
  352.6 4.9 fusion.131
  362.6 4.9 fusion.134
  367.8 3.4 fusion.135
  377.5 4.9 fusion.131
  387.5 4.9 fusion.134
  392.7 3.4 fusion.135
  402.4 4.9 fusion.131
  412.5 4.9 fusion.134
  417.6 3.4 fusion.135
  427.3 4.9 fusion.131
  437.4 4.9 fusion.134
  442.5 3.4 fusion.135
  452.2 4.9 fusion.131
  462.3 4.9 fusion.134
  467.4 3.4 fusion.135
  477.2 4.9 fusion.131
  487.2 4.9 fusion.134
  502.1 4.9 fusion.131
  512.1 4.9 fusion.134
  517.2 3.4 fusion.135
  527.0 4.9 fusion.131
  537.0 4.9 fusion.134
  551.9 4.9 fusion.131
  561.9 4.9 fusion.134
  567.1 3.4 fusion.135
  576.8 4.9 fusion.131
  586.8 4.9 fusion.134
  603.2 4.9 fusion.80
  611.5 3.5 fusion.60
  615.0 3.6 fusion.63
  618.8 29.5 %fusion.54 = f32[64,16,1024]{2,1,0:T(8,128)} fusion(bf16[64,2,63,1024]{3,0,2,1:T(8,128)(2,1)} %fusion.50, bf16[64,1,63,16]{2,3,1,0:T(8,128)(2,1)S(1)} %get-tuple-element.263, bf16[64,1,63,16]{2,3,1,0:T(8,128)(2,1)S(1)} %get-tuple-element.262), kind=kOutput, calls=%fused_computation.270 | convolution fusion | flops 264370176 | bytes 20967424 | tf_op jit(solution)/shard_map/fpbk,fpbx->fkx/dot_general | solution.py:139
  (767 shorter events, 171.7 us)
Async XLA Ops:
  7.2 289.7 %all-reduce.2.cloned.1.call-start = ((), (), s32[]{:S(2)}) async-start(), calls=%async_computation | async-start | bytes 4194304 | tf_op jit(solution)/shard_map/psum | solution.py:132
  32.1 21.1 %copy-start.5 = (f32[1024]{0:T(1024)S(1)}, f32[1024]{0:T(1024)}, u32[]{:S(2)}) copy-start(f32[1024]{0:T(1024)} %param.8) | copy-start | bytes 12292
  32.1 21.1 %copy-start.6 = (f32[1024]{0:T(1024)S(1)}, f32[1024]{0:T(1024)}, u32[]{:S(2)}) copy-start(f32[1024]{0:T(1024)} %param.7) | copy-start | bytes 12292
  138.2 2.2 copy-start.1
  142.4 150.6 %copy-start.2 = (f32[64,2,63,8]{0,3,2,1:T(8,128)S(1)}, f32[64,2,63,8]{0,3,2,1:T(8,128)}, u32[]{:S(2)}) copy-start(f32[64,2,63,8]{0,3,2,1:T(8,128)} %param.9) | copy-start | bytes 774148
  601.9 6.3 copy-start
  618.7 30.2 %copy-start.4 = (f32[64,8]{0,1:T(8,128)}, f32[64,8]{0,1:T(8,128)S(1)}, u32[]{:S(2)}) copy-start(f32[64,8]{0,1:T(8,128)S(1)} %copy.354) | copy-start | bytes 6148
  618.8 29.5 %copy-start.3 = (f32[64,2,63]{2,1,0:T(2,128)S(1)}, f32[64,2,63]{2,1,0:T(2,128)}, u32[]{:S(2)}) copy-start(f32[64,2,63]{2,1,0:T(2,128)} %broadcast_multiply_fusion.13) | copy-start | bytes 96772
Sparse Core Ops, SparseCore 0:
  142.5 154.3 all-reduce.1
